TPU v7x, 32 devices: a whole 2x2x4 slice. The times are simulated.
32 devices in a mesh: ctx: 8 (over z, x), head: 4 (over y, core).
Axes of the slice: x: 2, y: 2, z: 4, core: 2. Of those that a mesh axis runs over, the one named last changes fastest.
Arguments:
- queries: bfloat16 [1024, 4096], P('ctx', 'head'), may hold values from -24 to 24
- key_rows: bfloat16 [1024, 4096], P('ctx', 'head'), may hold values from -24 to 24
- value_rows: bfloat16 [1024, 4096], P('ctx', 'head'), may hold values from -6 to 6
- upstream: bfloat16 [1024, 6144], P('ctx', 'head'), may hold values from -6 to 6
- out_weight: bfloat16 [6144, 4096], P('ctx', 'head'), may hold values from -0.078125 to 0.078125
- group_ids: int32 [1024], replicated, may hold values from 0 to 7, never falling along the last dimension, each value on 1 to 256 neighbouring positions
Outputs:
- grad_queries: bfloat16 [1024, 4096], P('ctx', 'head')
- grad_keys: bfloat16 [1024, 4096], P('ctx', 'head')
- grad_values: bfloat16 [1024, 4096], P('ctx', 'head')
Inputs may be any that keep to these rules, and one draw needn't show every extreme that they name: `group_ids`: never falling along the tokens; each group number covers 1 to 256 consecutive tokens, one exactly 256.
All inputs are finite; a program needn't handle non-finite values.
Results may differ from a plain program's by a relative error of at most 0.025.
Values may be sent and summed in bfloat16 or wider, within the bound.
No kernel may reach another device: no remote copies, remote signals or barrier semaphores. Data moves between devices by JAX's collectives and lax.ppermute only.
A program may use at most 64 MiB of HBM per device.

v0:
```python
import jax
import jax.numpy as jnp
from jax import lax
from jax.sharding import PartitionSpec as P

HDIM = 128
masked_score = -1e30


def body(queries, key_rows, value_rows, upstream, out_weight, group_ids):
    rows_dev = queries.shape[0]
    heads_dev = queries.shape[1] // HDIM
    scaling = HDIM ** (-0.5)
    own_start = lax.axis_index("ctx") * rows_dev
    own_ids = lax.dynamic_slice_in_dim(group_ids, own_start, rows_dev, 0)
    upstream_full = lax.all_gather(upstream, "head", axis=1, tiled=True)
    grad_out = jnp.dot(
        upstream_full,
        lax.all_gather(out_weight, "ctx", axis=0, tiled=True),
        preferred_element_type=jnp.float32,
    ).astype(jnp.bfloat16)
    query_heads = queries.reshape(rows_dev, heads_dev, HDIM)
    grad_heads = grad_out.reshape(rows_dev, heads_dev, HDIM)
    key_heads = key_rows.reshape(rows_dev, heads_dev, HDIM)
    value_heads = value_rows.reshape(rows_dev, heads_dev, HDIM)
    stats_shape = (heads_dev, rows_dev)
    key_piece = lax.all_gather(key_rows, "ctx", axis=0, tiled=True)
    piece_rows = key_piece.shape[0]
    piece_ids = group_ids
    key_block = key_piece.reshape(piece_rows, heads_dev, HDIM)
    allowed = (piece_ids[None, :] <= own_ids[:, None])[None]
    run_max = jnp.full(stats_shape, masked_score, jnp.float32)
    scores = scaling * jnp.einsum(
        "qhd,khd->hqk", query_heads, key_block, preferred_element_type=jnp.float32
    )
    scores = jnp.where(allowed, scores, masked_score)
    new_max = jnp.maximum(run_max, jnp.max(scores, axis=2))
    weights = jnp.where(allowed, jnp.exp(scores - new_max[:, :, None]), 0.0)
    run_sum = jnp.sum(weights, axis=2)
    run_max, run_sum = (new_max, run_sum)
    log_total = run_max + jnp.log(run_sum)
    key_piece = lax.all_gather(key_rows, "ctx", axis=0, tiled=True)
    value_piece = lax.all_gather(value_rows, "ctx", axis=0, tiled=True)
    piece_rows = key_piece.shape[0]
    piece_ids = group_ids
    key_block = key_piece.reshape(piece_rows, heads_dev, HDIM)
    value_block = value_piece.reshape(piece_rows, heads_dev, HDIM)
    allowed = (piece_ids[None, :] <= own_ids[:, None])[None]
    scores = scaling * jnp.einsum(
        "qhd,khd->hqk", query_heads, key_block, preferred_element_type=jnp.float32
    )
    probs = jnp.where(allowed, jnp.exp(scores - log_total[:, :, None]), 0.0)
    probs_low = probs.astype(jnp.bfloat16)
    grad_probs = jnp.einsum(
        "qhd,khd->hqk", grad_heads, value_block, preferred_element_type=jnp.float32
    )
    mixed_low = (probs * grad_probs).astype(jnp.bfloat16)
    out_acc = jnp.einsum("hqk,khd->hqd", probs_low, value_block, preferred_element_type=jnp.float32)
    mixed_acc = jnp.einsum("hqk,khd->hqd", mixed_low, key_block, preferred_element_type=jnp.float32)
    plain_acc = jnp.einsum("hqk,khd->hqd", probs_low, key_block, preferred_element_type=jnp.float32)
    forward = (out_acc, mixed_acc, plain_acc)
    attn_out, mixed_acc, plain_acc = forward
    delta = jnp.einsum("qhd,hqd->hq", grad_heads.astype(jnp.float32), attn_out)
    grad_query = scaling * (mixed_acc - delta[:, :, None] * plain_acc)
    grad_queries = (
        grad_query.transpose(1, 0, 2).reshape(rows_dev, heads_dev * HDIM).astype(jnp.bfloat16)
    )
    all_lse, all_delta = (
        lax.all_gather(log_total.T, "ctx", axis=0, tiled=True),
        lax.all_gather(delta.T, "ctx", axis=0, tiled=True),
    )
    query_piece = lax.all_gather(queries, "ctx", axis=0, tiled=True)
    grad_piece = lax.all_gather(grad_out, "ctx", axis=0, tiled=True)
    piece_rows = query_piece.shape[0]
    piece_ids = group_ids
    piece_lse = all_lse.T
    piece_delta = all_delta.T
    query_block = query_piece.reshape(piece_rows, heads_dev, HDIM)
    grad_block = grad_piece.reshape(piece_rows, heads_dev, HDIM)
    allowed = (own_ids[None, :] <= piece_ids[:, None])[None]
    scores = scaling * jnp.einsum(
        "qhd,khd->hqk", query_block, key_heads, preferred_element_type=jnp.float32
    )
    probs = jnp.where(allowed, jnp.exp(scores - piece_lse[:, :, None]), 0.0)
    probs_low = probs.astype(jnp.bfloat16)
    grad_probs = jnp.einsum(
        "qhd,khd->hqk", grad_block, value_heads, preferred_element_type=jnp.float32
    )
    grad_scores = (probs * (grad_probs - piece_delta[:, :, None])).astype(jnp.bfloat16)
    value_grad = jnp.einsum(
        "hqk,qhd->hkd", probs_low, grad_block, preferred_element_type=jnp.float32
    )
    key_grad = jnp.einsum(
        "hqk,qhd->hkd", grad_scores, query_block, preferred_element_type=jnp.float32
    )
    key_grad, value_grad = (key_grad, value_grad)
    grad_keys = (
        (scaling * key_grad)
        .transpose(1, 0, 2)
        .reshape(rows_dev, heads_dev * HDIM)
        .astype(jnp.bfloat16)
    )
    grad_values = (
        value_grad.transpose(1, 0, 2).reshape(rows_dev, heads_dev * HDIM).astype(jnp.bfloat16)
    )
    return (grad_queries, grad_keys, grad_values)


def solution(mesh):
    in_specs = (
        P("ctx", "head"),
        P("ctx", "head"),
        P("ctx", "head"),
        P("ctx", "head"),
        P("ctx", "head"),
        P(),
    )
    out_specs = (P("ctx", "head"), P("ctx", "head"), P("ctx", "head"))
    return jax.shard_map(body, mesh=mesh, in_specs=in_specs, out_specs=out_specs, check_vma=False)
```

profile of v0, /device:TPU:0, one launch (start us, length us, event | category | flops | bytes accessed | tf_op | source)
XLA Modules:
  0.0 434.6 jit_solution(9773748842374155028)
XLA Ops:
  7.2 0.0 copy-start.6
  7.2 0.0 all-gather.9.cloned.1.call-start
  7.2 0.7 all-gather.9.cloned.1.call-update
  7.9 0.0 all-gather.11.cloned.1.call-start
  8.0 0.7 all-gather.11.cloned.1.call-update
  8.7 0.0 all-gather.7.cloned.1.call-start
  8.7 1.8 copy.18
  10.5 0.0 all-gather.7.cloned.1.call-update
  10.5 0.0 all-gather.15.cloned.1.call-start
  10.6 1.8 copy.21
  12.4 0.0 all-gather.15.cloned.1.call-update
  12.4 0.0 all-gather.13.cloned.1.call-start
  12.4 0.5 all-gather.13.cloned.1.call-update
  13.0 0.0 all-gather.17.cloned.1.call-start
  13.0 1.1 copy.41
  14.2 0.0 copy-done.6
  14.2 0.1 dynamic_slice.3
  14.2 0.1 broadcast_compare_fusion.1
  14.4 0.0 copy-start.4
  14.4 17.5 %all-gather.9.cloned.1.call-done = bf16[128,6144]{1,0:T(8,128)(2,1)} async-done(((bf16[128,1536]{1,0:T(8,128)(2,1)}), bf16[128,6144]{1,0:T(8,128)(2,1)}) %all-gather.9.cloned.1.call-update) | async-done | bytes 1572880 | tf_op jit(solution)/shard_map/all_gather | solution.py:16
  31.9 178.3 %all-gather.11.cloned.1.call-done = bf16[6144,1024]{1,0:T(8,128)(2,1)} async-done(((bf16[768,1024]{1,0:T(8,128)(2,1)}), bf16[6144,1024]{1,0:T(8,128)(2,1)}) %all-gather.11.cloned.1.call-update) | async-done | bytes 12582928 | tf_op jit(solution)/shard_map/all_gather | solution.py:19
  210.2 7.6 %convolution_convert_fusion = bf16[128,1024]{1,0:T(8,128)(2,1)} fusion(bf16[128,6144]{1,0:T(8,128)(2,1)} %all-gather.9.cloned.1.call-done, bf16[6144,1024]{1,0:T(8,128)(2,1)} %all-gather.11.cloned.1.call-done), kind=kOutput, calls=%fused_computation.28 | convolution fusion | flops 1610743808 | bytes 14417920 | tf_op jit(solution)/shard_map/dot_general | solution.py:17
  217.8 0.0 all-gather.17.cloned.1.call-update
  217.8 0.2 broadcast_compare_fusion
  218.0 43.4 %all-gather.7.cloned.1.call-done = bf16[1024,1024]{0,1:T(8,128)(2,1)} async-done(((bf16[128,1024]{0,1:T(8,128)(2,1)}), bf16[1024,1024]{0,1:T(8,128)(2,1)}) %all-gather.7.cloned.1.call-update) | async-done | bytes 2097168 | tf_op jit(solution)/shard_map/all_gather | solution.py:42
  261.4 0.0 copy-done.4
  261.4 0.0 copy-start.5
  261.4 2.7 select_reduce_fusion.1
  264.2 0.0 copy-start
  264.2 2.0 copy-done
  266.2 1.3 select_reduce_fusion
  267.5 31.1 %all_gather.30 = f32[1024,8]{0,1:T(8,128)S(1)} all-gather(f32[128,8]{0,1:T(8,128)S(1)} %bitcast.100), channel_id=1, replica_groups=mesh['ctx'=8,'head'=4] {'ctx'}, dimensions={0}, use_global_device_ids=true | all-gather | bytes 36864 | tf_op jit(solution)/shard_map/all_gather | solution.py:69
  298.6 13.9 %all-gather.15.cloned.1.call-done = bf16[1024,1024]{0,1:T(8,128)(2,1)} async-done(((bf16[128,1024]{0,1:T(8,128)(2,1)}), bf16[1024,1024]{0,1:T(8,128)(2,1)}) %all-gather.15.cloned.1.call-update) | async-done | bytes 2097168 | tf_op jit(solution)/shard_map/all_gather | solution.py:72
  312.5 0.0 copy-done.5
  312.5 4.4 %fusion.32 = f32[8,1024,128]{2,1,0:T(8,128)} fusion(bf16[1024,8,128]{0,2,1:T(8,128)(2,1)} %bitcast.85, bf16[128,1024]{1,0:T(8,128)(2,1)S(1)} %copy-done.5), kind=kOutput, calls=%fused_computation.32 | convolution fusion | flops 268435456 | bytes 6553600 | tf_op jit(solution)/shard_map/qhd,khd->hqk/dot_general | solution.py:81
  316.8 0.0 copy-start.1
  316.8 0.0 copy-start.3
  316.8 44.9 %all-gather.13.cloned.1.call-done = bf16[1024,1024]{1,0:T(8,128)(2,1)} async-done(((bf16[128,1024]{1,0:T(8,128)(2,1)}), bf16[1024,1024]{1,0:T(8,128)(2,1)}) %all-gather.13.cloned.1.call-update) | async-done | bytes 2097168 | tf_op jit(solution)/shard_map/all_gather | solution.py:43
  361.7 4.1 fusion.17
  365.9 0.0 copy-done.1
  365.9 0.4 multiply_reduce_fusion
  366.4 0.0 copy-done.3
  366.4 5.0 %fusion.20 = f32[128,8,128]{0,2,1:T(8,128)S(1)} fusion(bf16[1024,8,128]{0,2,1:T(8,128)(2,1)S(1)} %bitcast.88, f32[8,128,1024]{2,1,0:T(8,128)} %copy-done, f32[8,128]{1,0:T(8,128)S(1)} %log_add_fusion, pred[128,1024]{1,0:T(8,128)(4,1)S(1)} %broadcast_compare_fusion.1, bf16[1024,1024]{1,0:T(8,128)(2,1)} %all-gather.13.cloned.1.call-done, ...), kind=kOutput, calls=%fused_computation.22 | convolution fusion | flops 542113792 | bytes 9310208 | tf_op jit(solution)/shard_map/hqk,khd->hqd/dot_general | solution.py:59
  371.4 3.4 fusion.28
  374.8 0.9 copy.25
  375.6 31.3 %all_gather.32 = f32[1024,8]{0,1:T(8,128)S(1)} all-gather(f32[128,8]{0,1:T(8,128)S(1)} %copy.37), channel_id=1, replica_groups=mesh['ctx'=8,'head'=4] {'ctx'}, dimensions={0}, use_global_device_ids=true | all-gather | bytes 36864 | tf_op jit(solution)/shard_map/all_gather | solution.py:70
  406.9 5.4 %all-gather.17.cloned.1.call-done = bf16[1024,1024]{1,0:T(8,128)(2,1)} async-done(((bf16[128,1024]{1,0:T(8,128)(2,1)}), bf16[1024,1024]{1,0:T(8,128)(2,1)}) %all-gather.17.cloned.1.call-update) | async-done | bytes 2097168 | tf_op jit(solution)/shard_map/all_gather | solution.py:73
  412.4 3.9 copy.42
  416.3 0.0 copy-start.2
  416.3 3.9 fusion.29
  420.2 0.9 copy.27
  421.0 0.0 copy-done.2
  421.0 5.9 %fusion.27 = bf16[8,128,128]{1,2,0:T(8,128)(2,1)S(1)} fusion(bf16[1024,8,128]{0,2,1:T(8,128)(2,1)S(1)} %bitcast.86, f32[8,1024,128]{2,1,0:T(8,128)} %fusion.32, bf16[1024,8,128]{0,2,1:T(8,128)(2,1)} %bitcast.91, bf16[128,8,128]{0,2,1:T(8,128)(2,1)S(1)} %bitcast.93, f32[8,1024]{1,0:T(8,128)S(1)} %bitcast.99, f32[8,1024]{1,0:T(8,128)S(1)} %bitcast.98, ...), kind=kOutput, calls=%fused_computation.27 | convolution fusion | flops 543424512 | bytes 9109504 | tf_op jit(solution)/shard_map/hqk,qhd->hkd/dot_general | solution.py:93
  426.9 0.9 copy.26
  (4 shorter events, 0.1 us)
Async XLA Ops:
  7.2 7.0 %copy-start.6 = (s32[1024]{0:T(1024)S(1)}, s32[1024]{0:T(1024)}, u32[]{:S(2)}) copy-start(s32[1024]{0:T(1024)} %param.11) | copy-start | bytes 12292
  7.2 24.8 %all-gather.9.cloned.1.call-start = ((), (), s32[]{:S(2)}) async-start(), calls=%async_computation.1 | async-start | bytes 1966080 | tf_op jit(solution)/shard_map/all_gather | solution.py:16
  7.9 202.3 %all-gather.11.cloned.1.call-start = ((), (), s32[]{:S(2)}) async-start(), calls=%async_computation.2 | async-start | bytes 14155776 | tf_op jit(solution)/shard_map/all_gather | solution.py:19
  8.7 252.8 %all-gather.7.cloned.1.call-start = ((), (), s32[]{:S(2)}) async-start(), calls=%async_computation | async-start | bytes 2359296 | tf_op jit(solution)/shard_map/all_gather | solution.py:42
  10.5 301.9 %all-gather.15.cloned.1.call-start = ((), (), s32[]{:S(2)}) async-start(), calls=%async_computation.4 | async-start | bytes 2359296 | tf_op jit(solution)/shard_map/all_gather | solution.py:72
  12.4 349.4 %all-gather.13.cloned.1.call-start = ((), (), s32[]{:S(2)}) async-start(), calls=%async_computation.3 | async-start | bytes 2359296 | tf_op jit(solution)/shard_map/all_gather | solution.py:43
  13.0 399.4 %all-gather.17.cloned.1.call-start = ((), (), s32[]{:S(2)}) async-start(), calls=%async_computation.5 | async-start | bytes 2359296 | tf_op jit(solution)/shard_map/all_gather | solution.py:73
  14.4 247.0 %copy-start.4 = (bf16[128,1024]{1,0:T(8,128)(2,1)S(1)}, bf16[128,1024]{1,0:T(8,128)(2,1)}, u32[]{:S(2)}) copy-start(bf16[128,1024]{1,0:T(8,128)(2,1)} %param.6) | copy-start | bytes 786436
  261.4 51.0 %copy-start.5 = (bf16[128,1024]{1,0:T(8,128)(2,1)S(1)}, bf16[128,1024]{1,0:T(8,128)(2,1)}, u32[]{:S(2)}) copy-start(bf16[128,1024]{1,0:T(8,128)(2,1)} %param.7) | copy-start | bytes 786436
  264.2 2.0 copy-start
  316.8 49.0 %copy-start.1 = (bf16[128,1024]{1,0:T(8,128)(2,1)S(1)}, bf16[128,1024]{1,0:T(8,128)(2,1)}, u32[]{:S(2)}) copy-start(bf16[128,1024]{1,0:T(8,128)(2,1)} %convolution_convert_fusion) | copy-start | bytes 786436
  316.8 49.5 %copy-start.3 = (bf16[1024,1024]{0,1:T(8,128)(2,1)S(1)}, bf16[1024,1024]{0,1:T(8,128)(2,1)}, u32[]{:S(2)}) copy-start(bf16[1024,1024]{0,1:T(8,128)(2,1)} %all-gather.7.cloned.1.call-done) | copy-start | bytes 6291460
  416.3 4.7 %copy-start.2 = (bf16[1024,1024]{0,1:T(8,128)(2,1)S(1)}, bf16[1024,1024]{0,1:T(8,128)(2,1)}, u32[]{:S(2)}) copy-start(bf16[1024,1024]{0,1:T(8,128)(2,1)} %all-gather.15.cloned.1.call-done) | copy-start | bytes 6291460
Sparse Core Ops, SparseCore 0:
  9.5 22.3 all-gather.8
  34.1 176.0 all-gather.10
  212.9 48.5 all-gather.6
  263.9 48.4 all-gather.14
  314.4 47.2 all-gather.12
  364.3 48.0 all-gather.16
where the time goes:
time: 435 us
  waiting for transfers between devices  305 us (70%)
  blocking collectives  62.4 us (14%)
  matrix products  36.9 us (8%)
  between operations  14.2 us (3%)
  local copies, waits for them, and re-layouts  13.3 us (3%)
    all_gather x1, waiting for transfers between devices, body(): lax.all_gather(out_weight, 'ctx', axis=0, tiled=True)  178 us
    all_gather x1, waiting for transfers between devices, body(): value_piece = lax.all_gather(value_rows, 'ctx', axis=0, tiled=True)  44.9 us
    all_gather x1, waiting for transfers between devices, body(): key_piece = lax.all_gather(key_rows, 'ctx', axis=0, tiled=True)  43.4 us
    all_gather x1, blocking collectives, body(): lax.all_gather(delta.T, 'ctx', axis=0, tiled=True)  31.3 us
    all_gather x1, blocking collectives, body(): lax.all_gather(log_total.T, 'ctx', axis=0, tiled=True)  31.1 us
    all_gather x1, waiting for transfers between devices, body(): upstream_full = lax.all_gather(upstream, 'head', axis=1, tiled=True)  17.5 us
    all_gather x1, waiting for transfers between devices, body(): query_piece = lax.all_gather(queries, 'ctx', axis=0, tiled=True)  13.9 us
  transfers between devices with their start and end apart: 6, of which 6 were waited for; matrix products, arithmetic and copies ran while one was open for 8% of the time, Pallas kernels for 0%

commit v1 on v0

--- a/solution.py
+++ b/solution.py
@@ -66,7 +66,9 @@
         grad_query.transpose(1, 0, 2).reshape(rows_dev, heads_dev * HDIM).astype(jnp.bfloat16)
     )
     all_lse, all_delta = (
-        lax.all_gather(log_total.T, "ctx", axis=0, tiled=True),
+        jnp.concatenate(
+            lax.all_to_all(jnp.stack([log_total.T] * lax.axis_size("ctx")), "ctx", 0, 0), 0
+        ),
         lax.all_gather(delta.T, "ctx", axis=0, tiled=True),
     )
     query_piece = lax.all_gather(queries, "ctx", axis=0, tiled=True)

time: 435 us -> 436 us (level)
  blocking collectives: 62.4 us -> 31.3 us
  waiting for transfers between devices: 305 us -> 333 us
    all_gather x1 -> x0, blocking collectives: 31.1 us -> none  [body(): lax.all_gather(log_total.T, 'ctx', axis=0, tiled=True)]
    all_gather x1, waiting for transfers between devices: 13.9 us -> 41.4 us  [body(): query_piece = lax.all_gather(queries, 'ctx', axis=0, tiled=True)]
  transfers between devices with their start and end apart: 6 -> 7, of which waited for: 6 -> 6; matrix products, arithmetic and copies ran while one was open for 8% -> 9% of each run, Pallas kernels for 0% -> 0%
where the time goes in v1:
time: 436 us; the launch traced here: 435 us
  waiting for transfers between devices  333 us (76%)
  matrix products  36.9 us (8%)
  blocking collectives  31.3 us (7%)
  between operations  14.2 us (3%)
  local copies, waits for them, and re-layouts  14 us (3%)
    all_gather x1, waiting for transfers between devices, body(): lax.all_gather(out_weight, 'ctx', axis=0, tiled=True)  178 us
    all_gather x1, waiting for transfers between devices, body(): value_piece = lax.all_gather(value_rows, 'ctx', axis=0, tiled=True)  44.9 us
    all_gather x1, waiting for transfers between devices, body(): key_piece = lax.all_gather(key_rows, 'ctx', axis=0, tiled=True)  43.4 us
    all_gather x1, waiting for transfers between devices, body(): query_piece = lax.all_gather(queries, 'ctx', axis=0, tiled=True)  41.4 us
    all_gather x1, blocking collectives, body(): lax.all_gather(delta.T, 'ctx', axis=0, tiled=True)  31.3 us
    all_gather x1, waiting for transfers between devices, body(): upstream_full = lax.all_gather(upstream, 'head', axis=1, tiled=True)  17.5 us
  transfers between devices with their start and end apart: 7, of which 6 were waited for; matrix products, arithmetic and copies ran while one was open for 9% of the time, Pallas kernels for 0%

profile of v1, /device:TPU:0, one launch (start us, length us, event | category | flops | bytes accessed | tf_op | source)
XLA Modules:
  0.0 435.0 jit_solution(3788681493488493403)
XLA Ops:
  7.2 0.0 copy-start.6
  7.2 0.0 all-gather.9.cloned.1.call-start
  7.2 0.7 all-gather.9.cloned.1.call-update
  7.9 0.0 all-gather.11.cloned.1.call-start
  8.0 0.7 all-gather.11.cloned.1.call-update
  8.7 0.0 all-gather.7.cloned.1.call-start
  8.7 1.8 copy.18
  10.5 0.0 all-gather.7.cloned.1.call-update
  10.5 0.0 all-gather.15.cloned.1.call-start
  10.6 1.8 copy.21
  12.4 0.0 all-gather.15.cloned.1.call-update
  12.4 0.0 all-gather.13.cloned.1.call-start
  12.4 0.5 all-gather.13.cloned.1.call-update
  13.0 0.0 all-gather.17.cloned.1.call-start
  13.0 1.1 copy.41
  14.2 0.0 copy-done.6
  14.2 0.1 dynamic_slice.3
  14.2 0.1 broadcast_compare_fusion.1
  14.4 0.0 copy-start.4
  14.4 17.5 %all-gather.9.cloned.1.call-done = bf16[128,6144]{1,0:T(8,128)(2,1)} async-done(((bf16[128,1536]{1,0:T(8,128)(2,1)}), bf16[128,6144]{1,0:T(8,128)(2,1)}) %all-gather.9.cloned.1.call-update) | async-done | bytes 1572880 | tf_op jit(solution)/shard_map/all_gather | solution.py:16
  31.9 178.3 %all-gather.11.cloned.1.call-done = bf16[6144,1024]{1,0:T(8,128)(2,1)} async-done(((bf16[768,1024]{1,0:T(8,128)(2,1)}), bf16[6144,1024]{1,0:T(8,128)(2,1)}) %all-gather.11.cloned.1.call-update) | async-done | bytes 12582928 | tf_op jit(solution)/shard_map/all_gather | solution.py:19
  210.2 7.6 %convolution_convert_fusion = bf16[128,1024]{1,0:T(8,128)(2,1)} fusion(bf16[128,6144]{1,0:T(8,128)(2,1)} %all-gather.9.cloned.1.call-done, bf16[6144,1024]{1,0:T(8,128)(2,1)} %all-gather.11.cloned.1.call-done), kind=kOutput, calls=%fused_computation.28 | convolution fusion | flops 1610743808 | bytes 14417920 | tf_op jit(solution)/shard_map/dot_general | solution.py:17
  217.8 0.0 all-gather.17.cloned.1.call-update
  217.8 0.2 broadcast_compare_fusion
  218.0 43.4 %all-gather.7.cloned.1.call-done = bf16[1024,1024]{0,1:T(8,128)(2,1)} async-done(((bf16[128,1024]{0,1:T(8,128)(2,1)}), bf16[1024,1024]{0,1:T(8,128)(2,1)}) %all-gather.7.cloned.1.call-update) | async-done | bytes 2097168 | tf_op jit(solution)/shard_map/all_gather | solution.py:42
  261.4 0.0 copy-done.4
  261.4 0.0 copy-start.5
  261.4 2.7 select_reduce_fusion.1
  264.2 0.0 copy-start
  264.2 2.0 copy-done
  266.2 1.3 select_reduce_fusion
  267.5 0.6 stack.2
  268.1 3.3 all-to-all-start
  271.5 41.4 %all-gather.15.cloned.1.call-done = bf16[1024,1024]{0,1:T(8,128)(2,1)} async-done(((bf16[128,1024]{0,1:T(8,128)(2,1)}), bf16[1024,1024]{0,1:T(8,128)(2,1)}) %all-gather.15.cloned.1.call-update) | async-done | bytes 2097168 | tf_op jit(solution)/shard_map/all_gather | solution.py:74
  312.9 0.0 copy-done.5
  312.9 4.4 %fusion.32 = f32[8,1024,128]{2,1,0:T(8,128)} fusion(bf16[1024,8,128]{0,2,1:T(8,128)(2,1)} %bitcast.87, bf16[128,1024]{1,0:T(8,128)(2,1)S(1)} %copy-done.5), kind=kOutput, calls=%fused_computation.32 | convolution fusion | flops 268435456 | bytes 6553600 | tf_op jit(solution)/shard_map/qhd,khd->hqk/dot_general | solution.py:83
  317.2 0.0 copy-start.1
  317.2 0.0 copy-start.3
  317.2 44.9 %all-gather.13.cloned.1.call-done = bf16[1024,1024]{1,0:T(8,128)(2,1)} async-done(((bf16[128,1024]{1,0:T(8,128)(2,1)}), bf16[1024,1024]{1,0:T(8,128)(2,1)}) %all-gather.13.cloned.1.call-update) | async-done | bytes 2097168 | tf_op jit(solution)/shard_map/all_gather | solution.py:43
  362.2 4.1 fusion.17
  366.3 0.0 copy-done.1
  366.3 0.4 multiply_reduce_fusion
  366.8 0.0 copy-done.3
  366.8 5.0 %fusion.20 = f32[128,8,128]{0,2,1:T(8,128)S(1)} fusion(bf16[1024,8,128]{0,2,1:T(8,128)(2,1)S(1)} %bitcast.90, f32[8,128,1024]{2,1,0:T(8,128)} %copy-done, f32[8,128]{1,0:T(8,128)S(1)} %log_add_fusion, pred[128,1024]{1,0:T(8,128)(4,1)S(1)} %broadcast_compare_fusion.1, bf16[1024,1024]{1,0:T(8,128)(2,1)} %all-gather.13.cloned.1.call-done, ...), kind=kOutput, calls=%fused_computation.22 | convolution fusion | flops 542113792 | bytes 9310208 | tf_op jit(solution)/shard_map/hqk,khd->hqd/dot_general | solution.py:59
  371.8 3.4 fusion.28
  375.2 0.9 copy.25
  376.0 31.3 %all_gather.28 = f32[1024,8]{0,1:T(8,128)S(1)} all-gather(f32[128,8]{0,1:T(8,128)S(1)} %copy.37), channel_id=1, replica_groups=mesh['ctx'=8,'head'=4] {'ctx'}, dimensions={0}, use_global_device_ids=true | all-gather | bytes 36864 | tf_op jit(solution)/shard_map/all_gather | solution.py:72
  407.3 5.4 %all-gather.17.cloned.1.call-done = bf16[1024,1024]{1,0:T(8,128)(2,1)} async-done(((bf16[128,1024]{1,0:T(8,128)(2,1)}), bf16[1024,1024]{1,0:T(8,128)(2,1)}) %all-gather.17.cloned.1.call-update) | async-done | bytes 2097168 | tf_op jit(solution)/shard_map/all_gather | solution.py:75
  412.8 3.9 copy.42
  416.7 0.0 all-to-all-done
  416.7 0.0 copy-start.2
  416.7 3.9 fusion.29
  420.6 0.9 copy.27
  421.4 0.0 copy-done.2
  421.4 5.9 %fusion.27 = bf16[8,128,128]{1,2,0:T(8,128)(2,1)S(1)} fusion(bf16[1024,8,128]{0,2,1:T(8,128)(2,1)S(1)} %bitcast.88, f32[8,1024,128]{2,1,0:T(8,128)} %fusion.32, bf16[1024,8,128]{0,2,1:T(8,128)(2,1)} %bitcast.93, bf16[128,8,128]{0,2,1:T(8,128)(2,1)S(1)} %bitcast.95, f32[8,1024]{1,0:T(8,128)S(1)} %bitcast.99, f32[8,1024]{1,0:T(8,128)S(1)} %bitcast.101, ...), kind=kOutput, calls=%fused_computation.27 | convolution fusion | flops 543424512 | bytes 9109504 | tf_op jit(solution)/shard_map/hqk,qhd->hkd/dot_general | solution.py:95
  427.3 0.9 copy.26
  (4 shorter events, 0.1 us)
Async XLA Ops:
  7.2 7.0 %copy-start.6 = (s32[1024]{0:T(1024)S(1)}, s32[1024]{0:T(1024)}, u32[]{:S(2)}) copy-start(s32[1024]{0:T(1024)} %param.11) | copy-start | bytes 12292
  7.2 24.8 %all-gather.9.cloned.1.call-start = ((), (), s32[]{:S(2)}) async-start(), calls=%async_computation.2 | async-start | bytes 1966080 | tf_op jit(solution)/shard_map/all_gather | solution.py:16
  7.9 202.3 %all-gather.11.cloned.1.call-start = ((), (), s32[]{:S(2)}) async-start(), calls=%async_computation.3 | async-start | bytes 14155776 | tf_op jit(solution)/shard_map/all_gather | solution.py:19
  8.7 252.8 %all-gather.7.cloned.1.call-start = ((), (), s32[]{:S(2)}) async-start(), calls=%async_computation.1 | async-start | bytes 2359296 | tf_op jit(solution)/shard_map/all_gather | solution.py:42
  10.5 302.4 %all-gather.15.cloned.1.call-start = ((), (), s32[]{:S(2)}) async-start(), calls=%async_computation.5 | async-start | bytes 2359296 | tf_op jit(solution)/shard_map/all_gather | solution.py:74
  12.4 349.8 %all-gather.13.cloned.1.call-start = ((), (), s32[]{:S(2)}) async-start(), calls=%async_computation.4 | async-start | bytes 2359296 | tf_op jit(solution)/shard_map/all_gather | solution.py:43
  13.0 399.8 %all-gather.17.cloned.1.call-start = ((), (), s32[]{:S(2)}) async-start(), calls=%async_computation.6 | async-start | bytes 2359296 | tf_op jit(solution)/shard_map/all_gather | solution.py:75
  14.4 247.0 %copy-start.4 = (bf16[128,1024]{1,0:T(8,128)(2,1)S(1)}, bf16[128,1024]{1,0:T(8,128)(2,1)}, u32[]{:S(2)}) copy-start(bf16[128,1024]{1,0:T(8,128)(2,1)} %param.6) | copy-start | bytes 786436
  261.4 51.4 %copy-start.5 = (bf16[128,1024]{1,0:T(8,128)(2,1)S(1)}, bf16[128,1024]{1,0:T(8,128)(2,1)}, u32[]{:S(2)}) copy-start(bf16[128,1024]{1,0:T(8,128)(2,1)} %param.7) | copy-start | bytes 786436
  264.2 2.0 copy-start
  268.1 148.6 %all-to-all-start = ((f32[8,128,8]{1,2,0:T(8,128)}), f32[8,128,8]{1,2,0:T(8,128)S(1)}, u32[]{:S(2)}, u32[]{:S(2)}) async-start(f32[8,128,8]{1,2,0:T(8,128)} %stack.2), calls=%async_computation | async-start | bytes 65536 | tf_op jit(solution)/shard_map/all_to_all | solution.py:70
  317.2 49.0 %copy-start.1 = (bf16[128,1024]{1,0:T(8,128)(2,1)S(1)}, bf16[128,1024]{1,0:T(8,128)(2,1)}, u32[]{:S(2)}) copy-start(bf16[128,1024]{1,0:T(8,128)(2,1)} %convolution_convert_fusion) | copy-start | bytes 786436
  317.2 49.5 %copy-start.3 = (bf16[1024,1024]{0,1:T(8,128)(2,1)S(1)}, bf16[1024,1024]{0,1:T(8,128)(2,1)}, u32[]{:S(2)}) copy-start(bf16[1024,1024]{0,1:T(8,128)(2,1)} %all-gather.7.cloned.1.call-done) | copy-start | bytes 6291460
  416.7 4.7 %copy-start.2 = (bf16[1024,1024]{0,1:T(8,128)(2,1)S(1)}, bf16[1024,1024]{0,1:T(8,128)(2,1)}, u32[]{:S(2)}) copy-start(bf16[1024,1024]{0,1:T(8,128)(2,1)} %all-gather.15.cloned.1.call-done) | copy-start | bytes 6291460
Sparse Core Ops, SparseCore 0:
  9.5 22.3 all-gather.8
  34.1 176.0 all-gather.10
  212.9 48.5 all-gather.6
  263.9 48.9 all-gather.14
  314.8 47.2 all-gather.12
  364.7 48.0 all-gather.16
